TPU v7x, 32 devices: a whole 2x2x4 slice. The times are simulated.
32 devices in a mesh: dp: 2 (over y), seq: 4 (over z), weight: 4 (over x, core).
Axes of the slice: x: 2, y: 2, z: 4, core: 2. Of those that a mesh axis runs over, the one named last changes fastest.
Arguments:
- tokens: bfloat16 [96, 200, 512], P(('dp', 'seq', 'weight')), may hold values from -6 to 6
- valid: int32 [96, 200], P(('dp', 'seq', 'weight')), may hold values from 0 to 1, as said below
- experts: int32 [96, 200, 2], P(('dp', 'seq', 'weight')), may hold values from 0 to 31, as said below
- slots: int32 [96, 200, 2], P(('dp', 'seq', 'weight')), may hold values from 0 to 47, as said below
- ln1_gain: float32 [512], replicated, may hold values from 0.5 to 1.5
- ln1_bias: float32 [512], replicated, may hold values from -3 to 3
- w_qkv: bfloat16 [512, 1536], replicated, may hold values from -0.875 to 0.875
- w_out: bfloat16 [512, 512], replicated, may hold values from -2.5 to 2.5
- ln2_gain: float32 [512], replicated, may hold values from 0.5 to 1.5
- ln2_bias: float32 [512], replicated, may hold values from -3 to 3
- w_router: bfloat16 [512, 32], replicated, may hold values from -0.5 to 0.5
- w_in: bfloat16 [32, 512, 2048], P(None, None, 'weight'), may hold values from -0.25 to 0.25
- w_back: bfloat16 [32, 2048, 512], P(None, 'weight'), may hold values from -6 to 6
- cotangent: bfloat16 [96, 200, 512], P(('dp', 'seq', 'weight')), may hold values from -6 to 6
Outputs:
- output: bfloat16 [96, 200, 512], P(('dp', 'seq', 'weight'))
- grad_tokens: bfloat16 [96, 200, 512], P(('dp', 'seq', 'weight'))
- grad_ln1_gain: float32 [512], replicated
- grad_ln1_bias: float32 [512], replicated
- grad_qkv: float32 [512, 1536], replicated
- grad_out: float32 [512, 512], replicated
- grad_ln2_gain: float32 [512], replicated
- grad_ln2_bias: float32 [512], replicated
- grad_router: float32 [512, 32], replicated
- grad_in: float32 [32, 512, 2048], P(('dp', 'seq'), None, 'weight')
- grad_back: float32 [32, 2048, 512], P(('dp', 'seq'), 'weight')
- rms: float32 [3], replicated
Inputs may be any that keep to these rules, and one draw needn't show every extreme that they name: Each token, padding positions too, names 2 different experts. `valid`: exactly 3 positions of each image are 0. Within one device's tokens, taken image by image, position by position, and k = 0 before k = 1, slots[t, k] counts the earlier pairs of valid tokens that name the same expert, and is 47 where that count reaches 47; pairs of padding positions have 47. Every device has an expert that is named more than 47 times.
All inputs are finite; a program needn't handle non-finite values.
Results may differ from a plain program's by a relative error of at most 0.015.
Values may be sent and summed in bfloat16 or wider, within the bound.
No kernel may reach another device: no remote copies, remote signals or barrier semaphores. Data moves between devices by JAX's collectives and lax.ppermute only.
A program may use at most 320 MiB of HBM per device.

v0:
```python
import jax
import jax.numpy as jnp
from jax import lax
from jax.sharding import PartitionSpec as P

HEADS = 8
HEAD_DIM = 64
TOP = 2
VALID = 197
CAP = 47


def layer_norm(values, gain_row, shift_row):
    centre = jnp.mean(values, axis=-1, keepdims=True)
    offset = values - centre
    spread = jnp.mean(offset * offset, axis=-1, keepdims=True)
    return offset * lax.rsqrt(spread + 1e-06) * gain_row + shift_row


def head_scores(query_rows, key_rows, valid_keys, score_scale):
    raw_scores = (
        jnp.einsum("iqhd,ikhd->ihqk", query_rows, key_rows, preferred_element_type=jnp.float32)
        * score_scale
    )
    return jnp.where(valid_keys[:, None, None, :] > 0, raw_scores, -1e30)


def on_device(
    tokens,
    valid,
    experts,
    slots,
    ln1_gain,
    ln1_bias,
    w_qkv,
    w_out,
    ln2_gain,
    ln2_bias,
    w_router,
    w_in,
    w_back,
    cotangent,
):
    image_count, part_len, feature_width = tokens.shape
    seq_devices = lax.axis_size("seq")
    head_images = image_count * seq_devices
    token_count = image_count * part_len
    local_heads = HEADS // seq_devices
    expert_count = w_in.shape[0]
    dump_row = CAP * expert_count
    score_scale = HEAD_DIM ** (-0.5)
    valid_rows = valid.astype(jnp.float32).reshape(token_count, 1)
    inputs_f32 = tokens.reshape(token_count, feature_width).astype(jnp.float32)
    normed_one, norm_one_back = jax.vjp(layer_norm, inputs_f32, ln1_gain, ln1_bias)
    normed_low = (normed_one * valid_rows).astype(jnp.bfloat16)
    qkv_rows = jnp.dot(normed_low, w_qkv, preferred_element_type=jnp.float32).astype(jnp.bfloat16)
    qkv_rows = qkv_rows.reshape(image_count, part_len, 3, feature_width)
    valid_copies = jnp.broadcast_to(
        valid[:, :, None, None], (image_count, part_len, 1, seq_devices)
    )
    head_rows, key_valid = (
        lax.all_to_all(qkv_rows, "seq", split_axis=3, concat_axis=0, tiled=True),
        lax.all_to_all(valid_copies, "seq", split_axis=3, concat_axis=0, tiled=True),
    )
    key_valid = key_valid.reshape(head_images, part_len)
    head_rows = head_rows.reshape(head_images, part_len, 3, local_heads, HEAD_DIM)
    query_rows = head_rows[:, :, 0]
    key_rows = head_rows[:, :, 1]
    value_rows = head_rows[:, :, 2]
    scores = head_scores(query_rows, key_rows, key_valid, score_scale)
    row_max = jnp.max(scores, axis=-1, keepdims=True)
    expo_rows = jnp.exp(scores - row_max)
    expo_total = jnp.sum(expo_rows, axis=-1, keepdims=True)
    weights_low = (expo_rows / expo_total).astype(jnp.bfloat16)
    log_total = row_max + jnp.log(expo_total)
    context = jnp.einsum(
        "ihqk,ikhd->iqhd", weights_low, value_rows, preferred_element_type=jnp.float32
    ).astype(jnp.bfloat16)
    context = context.reshape(head_images, part_len, local_heads * HEAD_DIM)
    context_rows = lax.all_to_all(context, "seq", split_axis=0, concat_axis=2, tiled=True).reshape(
        token_count, feature_width
    )
    branch = jnp.dot(context_rows, w_out, preferred_element_type=jnp.float32) * valid_rows
    middle = inputs_f32 + branch
    normed_two, norm_two_back = jax.vjp(layer_norm, middle, ln2_gain, ln2_bias)
    routed = (normed_two * valid_rows).astype(jnp.bfloat16)
    logits = jnp.dot(routed, w_router, preferred_element_type=jnp.float32)
    router_probs = jax.nn.softmax(logits, axis=-1)
    expert_ids = experts.reshape(token_count, TOP)
    slot_ids = slots.reshape(token_count, TOP)
    chosen = (expert_ids[..., None] == jnp.arange(expert_count, dtype=jnp.int32)).astype(
        jnp.float32
    )
    gate_values = jnp.sum(router_probs[:, None, :] * chosen, axis=-1)
    flat_index = jnp.where(slot_ids < CAP, slot_ids * expert_count + expert_ids, dump_row).reshape(
        -1
    )
    token_index = jnp.repeat(jnp.arange(token_count, dtype=jnp.int32), TOP)
    owner = (
        jnp.full((dump_row + 1,), token_count, jnp.int32).at[flat_index].set(token_index)[:dump_row]
    )
    slot_gate = (
        jnp.zeros((dump_row + 1,), jnp.float32)
        .at[flat_index]
        .set(gate_values.reshape(-1))[:dump_row]
    )
    routed_ext = jnp.concatenate([routed, jnp.zeros((1, feature_width), jnp.bfloat16)], axis=0)
    buffer_rows = jnp.take(routed_ext, owner, axis=0).reshape(CAP, expert_count, feature_width)
    gathered = lax.all_gather(buffer_rows, "weight", axis=0, tiled=True)
    pre_act = jnp.einsum("ced,edf->cef", gathered, w_in, preferred_element_type=jnp.float32)
    hidden_f32, gelu_back = jax.vjp(jax.nn.gelu, pre_act)
    hidden = hidden_f32.astype(jnp.bfloat16)
    expert_out = lax.psum_scatter(
        jnp.einsum("cef,efd->ced", hidden, w_back, preferred_element_type=jnp.float32).astype(
            jnp.bfloat16
        ),
        "weight",
        scatter_dimension=0,
        tiled=True,
    ).astype(jnp.float32)
    out_table = jnp.concatenate(
        [expert_out.reshape(dump_row, feature_width), jnp.zeros((1, feature_width), jnp.float32)],
        axis=0,
    )
    picked = jnp.take(out_table, flat_index, axis=0).reshape(token_count, TOP, feature_width)
    mixture = jnp.sum(gate_values[..., None] * picked, axis=1)
    final_rows = middle + mixture
    output = final_rows.astype(jnp.bfloat16).reshape(image_count, part_len, feature_width)
    square_sums = jnp.stack(
        [
            jnp.sum(branch * branch),
            jnp.sum(mixture * mixture),
            jnp.sum(valid_rows * final_rows * final_rows),
        ]
    )
    grad_rows = cotangent.reshape(token_count, feature_width).astype(jnp.float32)
    grad_gates = jnp.sum(grad_rows[:, None, :] * picked, axis=-1)
    grad_ext = jnp.concatenate([grad_rows, jnp.zeros((1, feature_width), jnp.float32)], axis=0)
    grad_slots = (jnp.take(grad_ext, owner, axis=0) * slot_gate[:, None]).astype(jnp.bfloat16)
    grad_slots = grad_slots.reshape(CAP, expert_count, feature_width)
    grad_probs = jnp.sum(grad_gates[..., None] * chosen, axis=1)
    grad_logits = router_probs * (
        grad_probs - jnp.sum(router_probs * grad_probs, axis=-1, keepdims=True)
    )
    grad_router_part = jnp.dot(
        routed.astype(jnp.float32).T, grad_logits, precision=lax.Precision.HIGHEST
    )
    grad_routed = jnp.dot(
        grad_logits, w_router.astype(jnp.float32).T, precision=lax.Precision.HIGHEST
    )
    out_grads = lax.all_gather(grad_slots, "weight", axis=0, tiled=True)
    grad_hidden = jnp.einsum("ced,efd->cef", out_grads, w_back, preferred_element_type=jnp.float32)
    grad_pre = gelu_back(grad_hidden)[0].astype(jnp.bfloat16)
    grad_back_part = jnp.einsum(
        "cef,ced->efd", hidden, out_grads, preferred_element_type=jnp.float32
    )
    grad_in_part = jnp.einsum(
        "ced,cef->edf", gathered, grad_pre, preferred_element_type=jnp.float32
    )
    grad_buffer = lax.psum_scatter(
        jnp.einsum("cef,edf->ced", grad_pre, w_in, preferred_element_type=jnp.float32).astype(
            jnp.bfloat16
        ),
        "weight",
        scatter_dimension=0,
        tiled=True,
    ).astype(jnp.float32)
    grad_table = jnp.concatenate(
        [grad_buffer.reshape(dump_row, feature_width), jnp.zeros((1, feature_width), jnp.float32)],
        axis=0,
    )
    grad_routed = grad_routed + jnp.sum(
        jnp.take(grad_table, flat_index, axis=0).reshape(token_count, TOP, feature_width), axis=1
    )
    grad_in, grad_back = (
        lax.psum_scatter(
            grad_in_part.astype(jnp.bfloat16), ("dp", "seq"), scatter_dimension=0, tiled=True
        ).astype(jnp.float32),
        lax.psum_scatter(
            grad_back_part.astype(jnp.bfloat16), ("dp", "seq"), scatter_dimension=0, tiled=True
        ).astype(jnp.float32),
    )
    grad_mid_norm, grad_gain_two, grad_bias_two = norm_two_back(grad_routed * valid_rows)
    grad_middle = grad_rows + grad_mid_norm
    grad_branch = (grad_middle * valid_rows).astype(jnp.bfloat16)
    grad_out_part = jnp.einsum(
        "td,te->de", context_rows, grad_branch, preferred_element_type=jnp.float32
    )
    grad_context = jnp.einsum(
        "te,de->td", grad_branch, w_out, preferred_element_type=jnp.float32
    ).astype(jnp.bfloat16)
    grad_context = grad_context.reshape(image_count, part_len, feature_width)
    grad_heads = lax.all_to_all(grad_context, "seq", split_axis=2, concat_axis=0, tiled=True)
    grad_heads = grad_heads.reshape(head_images, part_len, local_heads, HEAD_DIM)
    weights_again = jnp.exp(head_scores(query_rows, key_rows, key_valid, score_scale) - log_total)
    grad_weights = jnp.einsum(
        "iqhd,ikhd->ihqk", grad_heads, value_rows, preferred_element_type=jnp.float32
    )
    row_delta = jnp.sum(weights_again * grad_weights, axis=-1, keepdims=True)
    grad_scores = (weights_again * (grad_weights - row_delta)).astype(jnp.bfloat16)
    grad_query = (
        jnp.einsum("ihqk,ikhd->iqhd", grad_scores, key_rows, preferred_element_type=jnp.float32)
        * score_scale
    )
    grad_keys = (
        jnp.einsum("ihqk,iqhd->ikhd", grad_scores, query_rows, preferred_element_type=jnp.float32)
        * score_scale
    )
    grad_values = jnp.einsum(
        "ihqk,iqhd->ikhd", weights_low, grad_heads, preferred_element_type=jnp.float32
    )
    grad_qkv_heads = jnp.stack([grad_query, grad_keys, grad_values], axis=2).astype(jnp.bfloat16)
    grad_qkv_heads = grad_qkv_heads.reshape(head_images, part_len, 3, local_heads * HEAD_DIM)
    grad_qkv_rows = lax.all_to_all(
        grad_qkv_heads, "seq", split_axis=0, concat_axis=3, tiled=True
    ).reshape(token_count, 3 * feature_width)
    grad_qkv_part = jnp.einsum(
        "td,te->de", normed_low, grad_qkv_rows, preferred_element_type=jnp.float32
    )
    grad_normed = jnp.einsum("te,de->td", grad_qkv_rows, w_qkv, preferred_element_type=jnp.float32)
    grad_in_norm, grad_gain_one, grad_bias_one = norm_one_back(grad_normed * valid_rows)
    grad_tokens = (
        (grad_middle + grad_in_norm)
        .astype(jnp.bfloat16)
        .reshape(image_count, part_len, feature_width)
    )
    norm_grads = jnp.stack([grad_gain_one, grad_bias_one, grad_gain_two, grad_bias_two])
    summed = lax.psum(
        (grad_qkv_part, grad_out_part, grad_router_part, norm_grads, square_sums),
        ("dp", "seq", "weight"),
    )
    total_images = (
        image_count * lax.axis_size("dp") * lax.axis_size("seq") * lax.axis_size("weight")
    )
    rms_values = jnp.sqrt(summed[4] / float(total_images * VALID * feature_width))
    return (
        output,
        grad_tokens,
        summed[3][0],
        summed[3][1],
        summed[0],
        summed[1],
        summed[3][2],
        summed[3][3],
        summed[2],
        grad_in,
        grad_back,
        rms_values,
    )


def solution(mesh):
    placed = (
        P(("dp", "seq", "weight"), None, None),
        P(("dp", "seq", "weight"), None),
        P(("dp", "seq", "weight"), None, None),
        P(("dp", "seq", "weight"), None, None),
        P(),
        P(),
        P(),
        P(),
        P(),
        P(),
        P(),
        P(None, None, "weight"),
        P(None, "weight", None),
        P(("dp", "seq", "weight"), None, None),
    )
    return jax.shard_map(
        on_device,
        mesh=mesh,
        in_specs=placed,
        out_specs=(
            P(("dp", "seq", "weight"), None, None),
            P(("dp", "seq", "weight"), None, None),
            P(),
            P(),
            P(),
            P(),
            P(),
            P(),
            P(),
            P(("dp", "seq"), None, "weight"),
            P(("dp", "seq"), "weight", None),
            P(),
        ),
        check_vma=False,
    )
```

profile of v0, /device:TPU:0, one launch (start us, length us, event | category | flops | bytes accessed | tf_op | source)
XLA Modules:
  0.0 1270.7 jit_solution(5230409070049920375)
XLA Ops:
  8.6 6.3 all-to-all-start.1
  25.9 7.0 copy.186
  32.9 5.1 all-to-all-start
  38.0 70.3 %all-to-all-done = bf16[3,200,3,512]{1,2,0,3:T(4,128)(2,1)} async-done(((bf16[3,200,3,512]{1,2,0,3:T(4,128)(2,1)}), bf16[3,200,3,512]{1,2,0,3:T(4,128)(2,1)}, u32[]{:S(2)}, u32[]{:S(2)}) %all-to-all-start) | async-done | bytes 1843232 | tf_op jit(solution)/shard_map/all_to_all | solution.py:62
  118.9 3.5 all-to-all-start.2
  123.2 6.4 scatter_custom_fusion
  129.7 8.6 all-to-all-done.2
  142.6 5.4 gather_fusion
  151.1 44.6 %all-gather.3.cloned.1.call-done = bf16[188,32,512]{2,1,0:T(8,128)(2,1)} async-done(((bf16[47,32,512]{2,1,0:T(8,128)(2,1)}), bf16[188,32,512]{2,1,0:T(8,128)(2,1)}) %all-gather.3.cloned.1.call-update) | async-done | bytes 6160400 | tf_op jit(solution)/shard_map/all_gather | solution.py:109
  195.8 19.8 %fusion.15 = f32[32,188,512]{2,1,0:T(8,128)} fusion(bf16[32,512,512]{2,1,0:T(8,128)(2,1)} %param.27, bf16[188,32,512]{2,1,0:T(8,128)(2,1)} %all-gather.3.cloned.1.call-done), kind=kOutput, calls=%fused_computation.30 | convolution fusion | flops 3154116608 | bytes 35258368 | tf_op jit(solution)/shard_map/ced,edf->cef/dot_general | solution.py:110
  215.6 15.8 %convert_bitcast_fusion.1 = bf16[188,32,512]{2,0,1:T(8,128)(2,1)} fusion(bf16[32,512,512]{2,1,0:T(8,128)(2,1)} %param.28, f32[32,188,512]{2,1,0:T(8,128)} %fusion.15), kind=kOutput, calls=%fused_computation.25 | convolution fusion | flops 3184918528 | bytes 35258368 | tf_op jit(solution)/shard_map/cef,efd->ced/dot_general | solution.py:114
  231.4 8.8 copy.199
  244.8 4.5 mul.340
  251.8 4.9 gather_fusion.1
  257.1 41.3 %reduce-scatter.5.cloned.1.call-done = bf16[47,32,512]{2,1,0:T(8,128)(2,1)} async-done(((bf16[188,32,512]{2,1,0:T(8,128)(2,1)}), bf16[47,32,512]{2,1,0:T(8,128)(2,1)}) %reduce-scatter.5.cloned.1.call-update) | async-done | bytes 1540112 | tf_op jit(solution)/shard_map/reduce_scatter | solution.py:113
  298.3 3.5 pad_convert_fusion.1
  301.8 6.8 gather_fusion.2
  308.6 4.3 multiply_reduce_fusion.1
  313.7 6.6 scatter_custom_fusion.1
  323.5 45.7 %all-gather.5.cloned.1.call-done = bf16[188,32,512]{2,1,0:T(8,128)(2,1)} async-done(((bf16[47,32,512]{2,1,0:T(8,128)(2,1)}), bf16[188,32,512]{2,1,0:T(8,128)(2,1)}) %all-gather.5.cloned.1.call-update) | async-done | bytes 6160400 | tf_op jit(solution)/shard_map/all_gather | solution.py:151
  369.2 29.1 %fusion.6 = bf16[188,32,512]{2,0,1:T(8,128)(2,1)} fusion(f32[32,188,512]{2,1,0:T(8,128)} %fusion.15, bf16[32,512,512]{2,1,0:T(8,128)(2,1)} %param.28, bf16[188,32,512]{2,1,0:T(8,128)(2,1)} %all-gather.5.cloned.1.call-done), kind=kOutput, calls=%fused_computation.14 | convolution fusion | flops 3215720448 | bytes 41418752 | tf_op jit(solution)/shard_map/ced,efd->cef/dot_general | solution.py:152
  398.3 12.7 convert_bitcast_fusion
  410.9 8.8 copy.203
  419.8 19.6 %convolution_convert_fusion.1 = bf16[32,512,512]{2,1,0:T(8,128)(2,1)} fusion(bf16[188,32,512]{2,0,1:T(8,128)(2,1)} %fusion.6, bf16[188,32,512]{2,1,0:T(8,128)(2,1)} %all-gather.3.cloned.1.call-done), kind=kOutput, calls=%fused_computation.23 | convolution fusion | flops 3162505216 | bytes 29097984 | tf_op jit(solution)/shard_map/ced,cef->edf/dot_general | solution.py:157
  439.5 20.6 %convolution_convert_fusion = bf16[32,512,512]{2,1,0:T(8,128)(2,1)} fusion(bf16[188,32,512]{2,1,0:T(8,128)(2,1)} %all-gather.5.cloned.1.call-done, f32[32,188,512]{2,1,0:T(8,128)} %fusion.15), kind=kOutput, calls=%fused_computation.22 | convolution fusion | flops 3190226944 | bytes 35258368 | tf_op jit(solution)/shard_map/cef,ced->efd/dot_general | solution.py:154
  460.2 4.1 reshape.345
  464.3 6.1 multiply_reduce_fusion.2
  470.3 7.6 reduce-scatter.7.cloned.1.call-done
  481.4 6.8 gather_fusion.3
  488.2 3.8 broadcast_select_fusion.1
  492.0 4.2 reshape.349
  496.3 5.7 reduce_sum.259
  502.1 4.5 multiply_reduce_fusion.3
  510.4 4.8 all-to-all-start.3
  516.0 51.4 %all-to-all-done.3 = bf16[3,200,512]{1,0,2:T(4,128)(2,1)S(1)} async-done(((bf16[3,200,512]{1,0,2:T(4,128)(2,1)}), bf16[3,200,512]{1,0,2:T(4,128)(2,1)S(1)}, u32[]{:S(2)}, u32[]{:S(2)}) %all-to-all-start.3) | async-done | bytes 614432 | tf_op jit(solution)/shard_map/all_to_all | solution.py:193
  575.4 4.7 multiply_reduce_fusion
  593.0 4.6 all-to-all-start.4
  603.6 78.8 %all-to-all-done.4 = bf16[12,200,3,128]{3,1,2,0:T(8,128)(2,1)} async-done(((bf16[12,200,3,128]{3,1,2,0:T(8,128)(2,1)}), bf16[12,200,3,128]{3,1,2,0:T(8,128)(2,1)}, u32[]{:S(2)}, u32[]{:S(2)}) %all-to-all-start.4) | async-done | bytes 1843232 | tf_op jit(solution)/shard_map/all_to_all | solution.py:214
  682.4 3.5 copy.212
  685.9 4.2 reshape.352
  690.1 4.6 fusion.54
  702.7 38.5 %all-reduce.4 = (f32[4,512]{1,0:T(4,128)S(1)}, f32[3]{0:T(128)S(1)}) all-reduce(f32[4,512]{1,0:T(4,128)S(1)} %pad_maximum_fusion.1, f32[3]{0:T(128)S(1)} %pad_maximum_fusion.2), channel_id=1, replica_groups=mesh['dp'=2,'seq'=4,'weight'=4] {'dp','seq','weight'}, use_global_device_ids=true, to_apply=%region_27.29 | all-reduce | flops 2051 | bytes 16408 | tf_op jit(solution)/shard_map/psum | solution.py:228
  745.0 80.8 %reduce-scatter.9.cloned.1.call-done = bf16[4,512,512]{2,1,0:T(8,128)(2,1)} async-done(((bf16[32,512,512]{2,1,0:T(8,128)(2,1)}), bf16[4,512,512]{2,1,0:T(8,128)(2,1)}) %reduce-scatter.9.cloned.1.call-update) | async-done | bytes 2097168 | tf_op jit(solution)/shard_map/reduce_scatter | solution.py:176
  825.7 4.2 convert_element_type.130
  829.9 278.0 %reduce-scatter.11.cloned.1.call-done = bf16[4,512,512]{2,1,0:T(8,128)(2,1)} async-done(((bf16[32,512,512]{2,1,0:T(8,128)(2,1)}), bf16[4,512,512]{2,1,0:T(8,128)(2,1)}) %reduce-scatter.11.cloned.1.call-update) | async-done | bytes 2097168 | tf_op jit(solution)/shard_map/reduce_scatter | solution.py:179
  1107.9 4.2 convert_element_type.132
  1112.1 146.1 %all-reduce.8.cloned.1.call-done = (f32[512,1536]{1,0:T(8,128)}, f32[512,512]{1,0:T(8,128)}, f32[512,32]{0,1:T(8,128)}) async-done(((f32[512,1536]{1,0:T(8,128)}, f32[512,512]{1,0:T(8,128)}, f32[512,32]{0,1:T(8,128)}), (f32[512,1536]{1,0:T(8,128)}, f32[512,512]{1,0:T(8,128)}, f32[512,32]{0,1:T(8,128)})) %all-reduce.8.cloned.1.call-update) | async-done | bytes 4259856 | tf_op jit(solution)/shard_map/psum | solution.py:228
  1258.2 3.8 copy.248
  (229 shorter events, 90.7 us)
Async XLA Ops:
  7.2 13.2 %copy-start = (bf16[512,1536]{1,0:T(8,128)(2,1)S(1)}, bf16[512,1536]{1,0:T(8,128)(2,1)}, u32[]{:S(2)}) copy-start(bf16[512,1536]{1,0:T(8,128)(2,1)} %param.22) | copy-start | bytes 4718596
  8.6 24.3 %all-to-all-start.1 = ((s32[3,200,1,4]{1,2,0,3:T(1,128)}), s32[3,200,1,4]{1,2,0,3:T(1,128)S(1)}, u32[]{:S(2)}, u32[]{:S(2)}) async-start(s32[3,200,1,4]{1,2,0,3:T(1,128)} %broadcast_in_dim.99), calls=%async_computation.1 | async-start | bytes 24576 | tf_op jit(solution)/shard_map/all_to_all | solution.py:63
  15.6 7.1 copy-start.39
  18.4 4.3 copy-start.48
  18.5 123.0 %copy-start.30 = (f32[600]{0:T(1024)}, f32[600]{0:T(1024)S(1)}, u32[]{:S(2)}) copy-start(f32[600]{0:T(1024)S(1)} %mul.318) | copy-start | bytes 7204
  32.9 75.4 %all-to-all-start = ((bf16[3,200,3,512]{1,2,0,3:T(4,128)(2,1)}), bf16[3,200,3,512]{1,2,0,3:T(4,128)(2,1)}, u32[]{:S(2)}, u32[]{:S(2)}) async-start(bf16[3,200,3,512]{1,2,0,3:T(4,128)(2,1)} %copy.186), calls=%async_computation | async-start | bytes 6291456 | tf_op jit(solution)/shard_map/all_to_all | solution.py:62
  38.0 75.5 %copy-start.26 = (pred[12,200]{1,0:T(8,128)(4,1)}, pred[12,200]{1,0:T(8,128)(4,1)S(1)}, u32[]{:S(2)}) copy-start(pred[12,200]{1,0:T(8,128)(4,1)S(1)} %gt.21) | copy-start | bytes 7204
  110.6 5.1 copy-start.8
  117.2 5.2 copy-start.43
  117.2 5.3 copy-start.56
  117.8 20.8 %copy-start.6 = (bf16[3,200,512]{2,1,0:T(8,128)(2,1)S(1)}, bf16[3,200,512]{2,1,0:T(8,128)(2,1)}, u32[]{:S(2)}) copy-start(bf16[3,200,512]{2,1,0:T(8,128)(2,1)} %param.16) | copy-start | bytes 1843204
  118.9 19.4 %all-to-all-start.2 = ((bf16[12,200,128]{2,1,0:T(8,128)(2,1)}), bf16[12,200,128]{2,1,0:T(8,128)(2,1)S(1)}, u32[]{:S(2)}, u32[]{:S(2)}) async-start(bf16[12,200,128]{2,1,0:T(8,128)(2,1)} %copy.192), calls=%async_computation.2 | async-start | bytes 1228800 | tf_op jit(solution)/shard_map/all_to_all | solution.py:80
  122.4 73.3 %all-gather.3.cloned.1.call-start = ((), (), s32[]{:S(2)}) async-start(), calls=%async_computation.9 | async-start | bytes 7700480 | tf_op jit(solution)/shard_map/all_gather | solution.py:109
  123.1 6.5 copy-start.54
  141.2 6.8 copy-start.28
  141.5 6.6 copy-start.37
  142.3 5.8 copy-start.35
  150.9 147.4 %reduce-scatter.5.cloned.1.call-start = ((), (), s32[]{:S(2)}) async-start(), calls=%async_computation.10 | async-start | bytes 7700480 | tf_op jit(solution)/shard_map/reduce_scatter | solution.py:113
  240.2 129.0 %all-gather.5.cloned.1.call-start = ((), (), s32[]{:S(2)}) async-start(), calls=%async_computation.11 | async-start | bytes 7700480 | tf_op jit(solution)/shard_map/all_gather | solution.py:151
  251.7 4.9 copy-start.25
  308.6 4.7 copy-start.44
  313.4 150.9 %copy-start.20 = (f32[600,32]{0,1:T(8,128)}, f32[600,32]{0,1:T(8,128)S(1)}, u32[]{:S(2)}) copy-start(f32[600,32]{0,1:T(8,128)S(1)} %get-tuple-element.23) | copy-start | bytes 230404
  323.4 154.5 %reduce-scatter.7.cloned.1.call-start = ((), (), s32[]{:S(2)}) async-start(), calls=%async_computation.12 | async-start | bytes 7700480 | tf_op jit(solution)/shard_map/reduce_scatter | solution.py:160
  419.8 405.9 %reduce-scatter.9.cloned.1.call-start = ((), (), s32[]{:S(2)}) async-start(), calls=%async_computation.13 | async-start | bytes 18874368 | tf_op jit(solution)/shard_map/reduce_scatter | solution.py:176
  439.5 668.5 %reduce-scatter.11.cloned.1.call-start = ((), (), s32[]{:S(2)}) async-start(), calls=%async_computation.14 | async-start | bytes 18874368 | tf_op jit(solution)/shard_map/reduce_scatter | solution.py:179
  496.3 5.8 copy-start.3
  496.3 5.8 copy-start.29
  496.3 5.8 copy-start.31
  496.3 5.8 copy-start.36
  496.3 5.8 copy-start.46
  502.1 4.5 copy-start.38
  508.5 6.7 copy-start.23
  510.4 56.9 %all-to-all-start.3 = ((bf16[3,200,512]{1,0,2:T(4,128)(2,1)}), bf16[3,200,512]{1,0,2:T(4,128)(2,1)S(1)}, u32[]{:S(2)}, u32[]{:S(2)}) async-start(bf16[3,200,512]{1,0,2:T(4,128)(2,1)} %copy.204), calls=%async_computation.5 | async-start | bytes 2097152 | tf_op jit(solution)/shard_map/all_to_all | solution.py:193
  569.7 5.7 copy-start.27
  575.4 4.7 slice-start
  575.4 4.7 slice-start.1
  592.9 4.9 copy-start.7
  592.9 4.9 copy-start.33
  592.9 4.9 copy-start.40
  592.9 4.9 copy-start.47
  593.0 4.9 copy-start.55
  593.0 4.9 copy-start.58
  593.0 8.0 copy-start.16
  593.0 89.4 %all-to-all-start.4 = ((bf16[12,200,3,128]{3,1,2,0:T(8,128)(2,1)}), bf16[12,200,3,128]{3,1,2,0:T(8,128)(2,1)}, u32[]{:S(2)}, u32[]{:S(2)}) async-start(bf16[12,200,3,128]{3,1,2,0:T(8,128)(2,1)} %pad_maximum_fusion), calls=%async_computation.6 | async-start | bytes 3686400 | tf_op jit(solution)/shard_map/all_to_all | solution.py:214
  597.6 660.7 %all-reduce.8.cloned.1.call-start = ((), (), s32[]{:S(2)}) async-start(), calls=%async_computation.15 | async-start | bytes 8519680 | tf_op jit(solution)/shard_map/psum | solution.py:228
  685.9 4.2 copy-start.18
  699.7 42.6 %copy-start.10 = (f32[600,512]{1,0:T(8,128)S(1)}, f32[600,512]{1,0:T(8,128)}, u32[]{:S(2)}) copy-start(f32[600,512]{1,0:T(8,128)} %copy-done.9) | copy-start | bytes 3686404
  1258.2 4.8 copy-start.34
  (25 other events, 51.0 us)
Sparse Core Ops, SparseCore 0:
  151.0 44.7 all-gather.2
  240.3 57.9 reduce-scatter.4
  323.6 45.5 all-gather.4
  419.9 57.9 reduce-scatter.6
  481.5 344.1 reduce-scatter.8
  829.3 278.5 reduce-scatter.10
  1115.1 143.0 all-reduce.7
where the time goes:
time: 1280 us; the launch traced here: 1270 us
  waiting for transfers between devices  853 us (67%)
  matrix products  155 us (12%)
  local copies, waits for them, and re-layouts  120 us (9%)
  other arithmetic  64.2 us (5%)
  blocking collectives  38.5 us (3%)
  starting transfers between devices  25 us (2%)
  between operations  15.2 us (1%)
    reduce_scatter x1, waiting for transfers between devices, on_device(): lax.psum_scatter(grad_back_part.astype(jnp.bfloat16), ('dp', 'seq'), scat...  278 us
    psum x1, waiting for transfers between devices, on_device(): lax.psum((grad_qkv_part, grad_out_part, grad_router_part, norm_grads, squ...  146 us
    reduce_scatter x1, waiting for transfers between devices, on_device(): lax.psum_scatter(grad_in_part.astype(jnp.bfloat16), ('dp', 'seq'), scatte...  80.8 us
    all_to_all x1, waiting for transfers between devices, on_device(): lax.all_to_all(grad_qkv_heads, 'seq', split_axis=0, concat_axis=3, tiled=...  78.8 us
    all_to_all x1, waiting for transfers between devices, on_device(): lax.all_to_all(qkv_rows, 'seq', split_axis=3, concat_axis=0, tiled=True)  70.3 us
    all_to_all x1, waiting for transfers between devices, on_device(): lax.all_to_all(grad_context, 'seq', split_axis=2, concat_axis=0, tiled=True)  51.4 us
    all_gather x1, waiting for transfers between devices, on_device(): out_grads = lax.all_gather(grad_slots, 'weight', axis=0, tiled=True)  45.7 us
    all_gather x1, waiting for transfers between devices, on_device(): gathered = lax.all_gather(buffer_rows, 'weight', axis=0, tiled=True)  44.6 us
  transfers between devices with their start and end apart: 12, of which 11 were waited for; matrix products, arithmetic and copies ran while one was open for 14% of the time, Pallas kernels for 0%

commit v1 on v0

v1 whole, which is shorter than its diff:
```python
import functools

import jax
import jax.numpy as jnp
from jax import lax
from jax.experimental import pallas as pl
from jax.experimental.pallas import tpu as pltpu
from jax.sharding import PartitionSpec as P

HEADS = 8
HEAD_DIM = 64
TOP = 2
VALID = 197
CAP = 47
ROWS = 48
EVERY = ("dp", "seq", "weight")
GROUP = ("dp", "seq")
PLANE = ("dp", "weight")
PAIR = 2 * HEAD_DIM
SCALE = HEAD_DIM ** (-0.5)
BF = jnp.bfloat16
F32 = jnp.float32
CURVE = 0.7978845608028654
CUBIC = 0.044715
VMEM = 60 * 1024 * 1024


def iota(shape, dim):
    return lax.broadcasted_iota(jnp.int32, shape, dim)


def mm(a, b, dims=((1,), (0,)), precision=None):
    return lax.dot_general(a, b, (dims, ((), ())), precision=precision, preferred_element_type=F32)


def mm_exact(a, b):
    return mm(a, b, precision=lax.Precision.HIGHEST)


def parts3(v):
    high = v.astype(BF)
    rest = v - high.astype(F32)
    mid = rest.astype(BF)
    low = (rest - mid.astype(F32)).astype(BF)
    return high, mid, low


def ln_stats(v):
    centre = jnp.mean(v, axis=-1, keepdims=True)
    off = v - centre
    spread = jnp.mean(off * off, axis=-1, keepdims=True)
    r = lax.rsqrt(spread + 1e-06)
    return off * r, r


def ln_back(u, n, r, gain):
    ug = u * gain
    return r * (
        ug - jnp.mean(ug, axis=-1, keepdims=True) - n * jnp.mean(ug * n, axis=-1, keepdims=True)
    )


def one_hot_rows(index_ref, first_row, row_count):
    width = index_ref.shape[-1]
    rows = iota((row_count, width), 0) + first_row
    hit = (rows == index_ref[0:1, :]) | (rows == index_ref[1:2, :])
    return jnp.where(hit, 1.0, 0.0).astype(BF)


def one_hot_tokens(index, row_count):
    rows = iota((index.shape[0], row_count), 1)
    hit = (rows == index[:, 0:1]) | (rows == index[:, 1:2])
    return jnp.where(hit, 1.0, 0.0).astype(BF)


def head_masks():
    lane = iota((1, PAIR), 1)
    first = jnp.where(lane < HEAD_DIM, 1.0, 0.0)
    return first.astype(BF), (1.0 - first).astype(BF)


def send_kernel(index_ref, rows_ref, out_ref, flat_ref, *, images, length, chunk):
    flat_ref[...] = jnp.zeros(flat_ref.shape, F32)
    for i in range(images):
        flat_ref[i * length : (i + 1) * length, :] = rows_ref[i].astype(F32)
    scatter_rows(index_ref, flat_ref, out_ref, chunk)


def scatter_rows(index_ref, flat_ref, out_ref, chunk):
    flat = flat_ref[...].astype(BF)
    blocks = out_ref.shape[0]
    width = out_ref.shape[2]

    def body(j, carry):
        hot = one_hot_rows(index_ref, j * (chunk * ROWS), chunk * ROWS)
        out = mm(hot, flat).astype(BF)
        out_ref[pl.ds(j * chunk, chunk)] = out.reshape(chunk, ROWS, width)
        return carry

    lax.fori_loop(0, blocks // chunk, body, 0)


def forward_kernel(
    x_ref,
    col_ref,
    row_ref,
    index_ref,
    gain1_ref,
    bias1_ref,
    w_qkv_ref,
    w_out_ref,
    gain2_ref,
    bias2_ref,
    w_router_ref,
    qkv_ref,
    ctx_ref,
    mid_ref,
    buf_ref,
    square_ref,
    flat_ref,
    gate_ref,
    *,
    images,
    length,
    experts,
    chunk,
):
    i = pl.program_id(0)
    width = x_ref.shape[2]

    @pl.when(i == 0)
    def _():
        flat_ref[...] = jnp.zeros(flat_ref.shape, F32)
        gate_ref[...] = jnp.zeros(gate_ref.shape, F32)
        square_ref[...] = jnp.zeros(square_ref.shape, F32)

    x = x_ref[0].astype(F32)
    m = col_ref[0][:, 4:5].astype(F32)
    n1, _ = ln_stats(x)
    a1 = ((n1 * gain1_ref[...] + bias1_ref[...]) * m).astype(BF)
    qkv_ref[0] = mm(a1, w_qkv_ref[...]).astype(BF)
    key_ok = row_ref[0][4:5, :] > 0
    masks = head_masks()
    lane = iota((length, PAIR), 1)
    for j in range(HEADS // 2):
        q = qkv_ref[0, :, j * PAIR : (j + 1) * PAIR]
        k = qkv_ref[0, :, width + j * PAIR : width + (j + 1) * PAIR]
        v = qkv_ref[0, :, 2 * width + j * PAIR : 2 * width + (j + 1) * PAIR]
        halves = []
        for mask in masks:
            s = mm(q * mask, k, ((1,), (1,))) * SCALE
            s = jnp.where(key_ok, s, -1e30)
            e = jnp.exp(s - jnp.max(s, axis=-1, keepdims=True))
            p = (e / jnp.sum(e, axis=-1, keepdims=True)).astype(BF)
            halves.append(mm(p, v))
        ctx_ref[0, :, j * PAIR : (j + 1) * PAIR] = jnp.where(
            lane < HEAD_DIM, halves[0], halves[1]
        ).astype(BF)
    att = mm(ctx_ref[0], w_out_ref[...]) * m
    square_ref[...] += jnp.sum(att * att, axis=0, keepdims=True)
    h = x + att
    mid_ref[0] = h
    n2, _ = ln_stats(h)
    a2 = ((n2 * gain2_ref[...] + bias2_ref[...]) * m).astype(BF)
    flat_ref[pl.ds(pl.multiple_of(i * length, 8), length), :] = a2.astype(F32)
    logits = mm(a2, w_router_ref[...])
    z = jnp.exp(logits - jnp.max(logits, axis=-1, keepdims=True))
    probs = z / jnp.sum(z, axis=-1, keepdims=True)
    expert_lane = iota((length, experts), 1)
    slot_lane = iota((length, 128), 1)
    expert_row = iota((experts, length), 0)
    for k in range(TOP):
        expert = col_ref[0][:, k : k + 1]
        slot = col_ref[0][:, TOP + k : TOP + k + 1]
        gate = jnp.sum(jnp.where(expert_lane == expert, probs, 0.0), axis=-1, keepdims=True)
        placed = jnp.where((slot_lane == slot) & (slot < CAP), gate, 0.0)
        mine = jnp.where(expert_row == row_ref[0][k : k + 1, :], 1.0, 0.0)
        gate_ref[...] += mm_exact(mine, placed)

    @pl.when(i == images - 1)
    def _():
        base = images * length
        high, mid, low = parts3(gate_ref[...])
        flat_ref[base : base + experts, 0:128] = high.astype(F32)
        flat_ref[base : base + experts, 128:256] = mid.astype(F32)
        flat_ref[base : base + experts, 256:384] = low.astype(F32)
        scatter_rows(index_ref, flat_ref, buf_ref, chunk)


def block_gates(block):
    count = block.shape[0]
    last = jnp.where(iota((count, ROWS, 1), 1) == CAP, block[:, :, 0:384].astype(F32), 0.0)
    row = jnp.sum(last, axis=1, keepdims=True)
    gates = row[:, :, 0:128] + row[:, :, 128:256] + row[:, :, 256:384]
    same = iota((count, ROWS, 128), 1) == iota((count, ROWS, 128), 2)
    return jnp.sum(jnp.where(same, gates, 0.0), axis=-1, keepdims=True)


def with_last_row(block, values):
    count, _, width = block.shape
    same = iota((count, ROWS, 128), 1) == iota((count, ROWS, 128), 2)
    row = jnp.sum(jnp.where(same, values, 0.0), axis=1, keepdims=True)
    high, mid, low = parts3(row)
    zero = jnp.zeros((count, 1, width - 384), F32)
    row = jnp.concatenate([high.astype(F32), mid.astype(F32), low.astype(F32), zero], axis=2)
    return jnp.where(iota((count, ROWS, 1), 1) == CAP, row, block).astype(BF)


def gelu_parts(pre):
    square = pre * pre
    t = jnp.tanh(CURVE * pre * (1.0 + CUBIC * square))
    half = 0.5 * (1.0 + t)
    slope = half + 0.5 * pre * (1.0 - t * t) * (CURVE * (1.0 + 3.0 * CUBIC * square))
    return pre * half, slope


def expert_kernel(
    rows_ref,
    dy_ref,
    w_in_ref,
    w_back_ref,
    grad_rows_ref,
    gated_ref,
    rows_out_ref,
    grad_out_ref,
    hidden_ref,
    grad_pre_ref,
):
    count, _, width = rows_ref.shape
    total = count * ROWS
    pieces = w_in_ref.shape[0]
    piece = w_in_ref.shape[2]
    block = rows_ref[...]
    gates = block_gates(block)
    rows = jnp.where(iota((count, ROWS, 1), 1) == CAP, 0.0, block.astype(F32)).astype(BF)
    rows = rows.reshape(total, width)
    rows_out_ref[...] = rows
    dy = dy_ref[...].astype(F32)
    grad_out = (gates * dy).astype(BF).reshape(total, width)
    grad_out_ref[...] = grad_out
    out = jnp.zeros((total, width), F32)
    grad_rows = jnp.zeros((total, width), F32)
    for q in range(pieces):
        pre = mm(rows, w_in_ref[q])
        hidden, slope = gelu_parts(pre)
        hidden = hidden.astype(BF)
        hidden_ref[:, q * piece : (q + 1) * piece] = hidden
        out = out + mm(hidden, w_back_ref[q])
        grad_pre = (mm(grad_out, w_back_ref[q], ((1,), (1,))) * slope).astype(BF)
        grad_pre_ref[:, q * piece : (q + 1) * piece] = grad_pre
        grad_rows = grad_rows + mm(grad_pre, w_in_ref[q], ((1,), (1,)))
    out = out.reshape(count, ROWS, width)
    grad_gate = jnp.sum(dy * out, axis=-1, keepdims=True)
    gated_ref[...] = (gates * out).astype(BF)
    grad_rows_ref[...] = with_last_row(grad_rows.reshape(count, ROWS, width), grad_gate)


def expert_weights_kernel(rows_ref, grad_out_ref, hidden_ref, grad_pre_ref, out_ref):
    width = rows_ref.shape[1]
    piece = hidden_ref.shape[1]
    out_ref[0, 0:width, :] = mm(rows_ref[...], grad_pre_ref[...], ((0,), (0,))).astype(BF)
    out_ref[0, width : width + piece, :] = mm(
        hidden_ref[...], grad_out_ref[...], ((0,), (0,))
    ).astype(BF)


def backward_kernel(
    back_ref,
    x_ref,
    mid_ref,
    dy_ref,
    qkv_ref,
    ctx_ref,
    col_ref,
    gain1_ref,
    bias1_ref,
    w_qkv_ref,
    w_out_ref,
    gain2_ref,
    bias2_ref,
    w_router_ref,
    grad_x_ref,
    weights_ref,
    norms_ref,
    sum_qkv_ref,
    sum_out_ref,
    sum_router_ref,
    grad_gate_ref,
    dqkv_ref,
    *,
    images,
    length,
    experts,
):
    i = pl.program_id(0)
    width = x_ref.shape[2]
    total = experts * ROWS

    @pl.when(i == 0)
    def _():
        sum_qkv_ref[...] = jnp.zeros(sum_qkv_ref.shape, F32)
        sum_out_ref[...] = jnp.zeros(sum_out_ref.shape, F32)
        sum_router_ref[...] = jnp.zeros(sum_router_ref.shape, F32)
        norms_ref[...] = jnp.zeros(norms_ref.shape, F32)
        last = iota((experts, total), 0) * ROWS + CAP == iota((experts, total), 1)
        picked = mm(jnp.where(last, 1.0, 0.0).astype(BF), back_ref[:, 0:384])
        grad_gate_ref[...] = picked[:, 0:128] + picked[:, 128:256] + picked[:, 256:384]

    col = col_ref[0]
    m = col[:, 4:5].astype(F32)
    x = x_ref[0].astype(F32)
    dy = dy_ref[0].astype(F32)
    n2, r2 = ln_stats(mid_ref[0])
    a2 = ((n2 * gain2_ref[...] + bias2_ref[...]) * m).astype(BF)
    logits = mm(a2, w_router_ref[...])
    z = jnp.exp(logits - jnp.max(logits, axis=-1, keepdims=True))
    probs = z / jnp.sum(z, axis=-1, keepdims=True)
    expert_lane = iota((length, experts), 1)
    slot_lane = iota((length, 128), 1)
    grad_probs = jnp.zeros((length, experts), F32)
    for k in range(TOP):
        slot = col[:, TOP + k : TOP + k + 1]
        mine = jnp.where(expert_lane == col[:, k : k + 1], 1.0, 0.0)
        table = mm_exact(mine, grad_gate_ref[...])
        grad_gate = jnp.sum(
            jnp.where((slot_lane == slot) & (slot < CAP), table, 0.0), axis=-1, keepdims=True
        )
        grad_probs = grad_probs + mine * grad_gate
    grad_logits = probs * (grad_probs - jnp.sum(probs * grad_probs, axis=-1, keepdims=True))
    high = grad_logits.astype(BF)
    low = (grad_logits - high.astype(F32)).astype(BF)
    sum_router_ref[...] += mm(a2, high, ((0,), (0,))) + mm(a2, low, ((0,), (0,)))
    grad_a2 = mm(one_hot_tokens(col[:, 6:8], total), back_ref[...])
    grad_a2 = grad_a2 + mm(high, w_router_ref[...], ((1,), (1,)))
    grad_a2 = grad_a2 + mm(low, w_router_ref[...], ((1,), (1,)))
    up2 = grad_a2 * m
    norms_ref[2:3, :] += jnp.sum(up2 * n2, axis=0, keepdims=True)
    norms_ref[3:4, :] += jnp.sum(up2, axis=0, keepdims=True)
    grad_mid = dy + ln_back(up2, n2, r2, gain2_ref[...])
    grad_att = (grad_mid * m).astype(BF)
    sum_out_ref[...] += mm(ctx_ref[0], grad_att, ((0,), (0,)))
    grad_ctx = mm(grad_att, w_out_ref[...], ((1,), (1,))).astype(BF)
    masks = head_masks()
    for j in range(HEADS // 2):
        q = qkv_ref[0, :, j * PAIR : (j + 1) * PAIR]
        k = qkv_ref[0, :, width + j * PAIR : width + (j + 1) * PAIR]
        v = qkv_ref[0, :, 2 * width + j * PAIR : 2 * width + (j + 1) * PAIR]
        g = grad_ctx[:, j * PAIR : (j + 1) * PAIR]
        dq = jnp.zeros((length, PAIR), F32)
        dk = jnp.zeros((length, PAIR), F32)
        dv = jnp.zeros((length, PAIR), F32)
        for mask in masks:
            qm = q * mask
            gm = g * mask
            s = mm(k, qm, ((1,), (1,))) * SCALE
            s = jnp.where(m > 0, s, -1e30)
            e = jnp.exp(s - jnp.max(s, axis=0, keepdims=True))
            p = e / jnp.sum(e, axis=0, keepdims=True)
            dp = mm(v, gm, ((1,), (1,)))
            ds = (p * (dp - jnp.sum(p * dp, axis=0, keepdims=True))).astype(BF)
            dv = dv + mm(p.astype(BF), gm)
            dk = dk + mm(ds, qm)
            dq = dq + mm(ds, k * mask, ((0,), (0,)))
        dqkv_ref[:, j * PAIR : (j + 1) * PAIR] = (dq * SCALE).astype(BF)
        dqkv_ref[:, width + j * PAIR : width + (j + 1) * PAIR] = (dk * SCALE).astype(BF)
        dqkv_ref[:, 2 * width + j * PAIR : 2 * width + (j + 1) * PAIR] = dv.astype(BF)
    n1, r1 = ln_stats(x)
    a1 = ((n1 * gain1_ref[...] + bias1_ref[...]) * m).astype(BF)
    dqkv = dqkv_ref[...]
    sum_qkv_ref[...] += mm(a1, dqkv, ((0,), (0,)))
    up1 = mm(dqkv, w_qkv_ref[...], ((1,), (1,))) * m
    norms_ref[0:1, :] += jnp.sum(up1 * n1, axis=0, keepdims=True)
    norms_ref[1:2, :] += jnp.sum(up1, axis=0, keepdims=True)
    grad_x_ref[0] = (grad_mid + ln_back(up1, n1, r1, gain1_ref[...])).astype(BF)

    @pl.when(i == images - 1)
    def _():
        weights_ref[:, 0 : 3 * width] = sum_qkv_ref[...].astype(BF)
        weights_ref[:, 3 * width : 4 * width] = sum_out_ref[...].astype(BF)
        weights_ref[:, 4 * width : 4 * width + experts] = sum_router_ref[...].astype(BF)


def final_kernel(back_ref, mid_ref, col_ref, out_ref, squares_ref):
    i = pl.program_id(0)

    @pl.when(i == 0)
    def _():
        squares_ref[...] = jnp.zeros(squares_ref.shape, F32)

    col = col_ref[0]
    m = col[:, 4:5].astype(F32)
    moe = mm(one_hot_tokens(col[:, 6:8], back_ref.shape[0]), back_ref[...])
    y = mid_ref[0] + moe
    out_ref[0] = y.astype(BF)
    squares_ref[0:1, :] += jnp.sum(moe * moe, axis=0, keepdims=True)
    squares_ref[1:2, :] += jnp.sum(m * y * y, axis=0, keepdims=True)


def whole(array):
    zeros = (0,) * array.ndim
    return pl.BlockSpec(array.shape, lambda *_: zeros)


def whole_out(shape):
    zeros = (0,) * len(shape)
    return pl.BlockSpec(shape, lambda *_: zeros)


def per_image(array):
    rest = array.shape[1:]
    zeros = (0,) * len(rest)
    return pl.BlockSpec((1,) + rest, lambda i: (i,) + zeros)


PARAMS = pltpu.CompilerParams(vmem_limit_bytes=VMEM)


def exchange(v, axes):
    return lax.all_to_all(v, axes, split_axis=0, concat_axis=0, tiled=True)


def experts_here(rows, dy_rows, w_in_all, w_back_all):
    w_in, w_back = w_in_all, w_back_all
    devices, _, width = rows.shape
    pieces, _, piece = w_in.shape
    step = 8 if devices % 8 == 0 else 1
    total = devices * ROWS
    block3 = pl.BlockSpec((step, ROWS, width), lambda i: (i, 0, 0))
    block2 = pl.BlockSpec((step * ROWS, width), lambda i: (i, 0))
    wide2 = pl.BlockSpec((step * ROWS, pieces * piece), lambda i: (i, 0))
    grad_rows, gated, rows_low, grad_out, hidden, grad_pre = pl.pallas_call(
        expert_kernel,
        grid=(devices // step,),
        in_specs=[block3, block3, whole(w_in), whole(w_back)],
        out_specs=[block3, block3, block2, block2, wide2, wide2],
        out_shape=[
            jax.ShapeDtypeStruct((devices, ROWS, width), BF),
            jax.ShapeDtypeStruct((devices, ROWS, width), BF),
            jax.ShapeDtypeStruct((total, width), BF),
            jax.ShapeDtypeStruct((total, width), BF),
            jax.ShapeDtypeStruct((total, pieces * piece), BF),
            jax.ShapeDtypeStruct((total, pieces * piece), BF),
        ],
        compiler_params=PARAMS,
        name="experts",
    )(rows, dy_rows, w_in, w_back)
    column = pl.BlockSpec((total, piece), lambda q: (0, q))
    grads = pl.pallas_call(
        expert_weights_kernel,
        grid=(pieces,),
        in_specs=[whole(rows_low), whole(grad_out), column, column],
        out_specs=pl.BlockSpec((1, width + piece, width), lambda q: (q, 0, 0)),
        out_shape=jax.ShapeDtypeStruct((pieces, width + piece, width), BF),
        compiler_params=PARAMS,
        name="expert_weights",
    )(rows_low, grad_out, hidden, grad_pre)
    return grad_rows, gated, grads


def experts_split(rows, dy_rows, w_in, w_back, groups):
    local, width, _ = w_in.shape
    block = rows.reshape(groups * local, ROWS, width)
    last = block[:, CAP, :384].astype(F32).reshape(-1, 3, 128).sum(axis=1)
    gates = last[:, :ROWS, None]
    rows = block.at[:, CAP].set(0).reshape(groups, local, ROWS, width)
    dy = dy_rows.reshape(groups * local, ROWS, width).astype(F32)
    grad_out = (gates * dy).astype(BF).reshape(groups, local, ROWS, width)
    rows_all = lax.all_gather(rows, "weight", axis=0, tiled=True)
    grad_all = lax.all_gather(grad_out, "weight", axis=0, tiled=True)
    pre = jnp.einsum("gecd,edf->gecf", rows_all, w_in, preferred_element_type=F32)
    hidden, slope = gelu_parts(pre)
    hidden = hidden.astype(BF)
    out = jnp.einsum("gecf,efd->gecd", hidden, w_back, preferred_element_type=F32)
    out = lax.psum_scatter(out.astype(BF), "weight", scatter_dimension=0, tiled=True)
    out = out.astype(F32).reshape(groups * local, ROWS, width)
    grad_hidden = jnp.einsum("gecd,efd->gecf", grad_all, w_back, preferred_element_type=F32)
    grad_pre = (grad_hidden * slope).astype(BF)
    grad_rows = jnp.einsum("gecf,edf->gecd", grad_pre, w_in, preferred_element_type=F32)
    grad_rows = lax.psum_scatter(
        grad_rows.astype(BF), "weight", scatter_dimension=0, tiled=True
    ).reshape(groups * local, ROWS, width)
    grad_in = jnp.einsum("gecd,gecf->edf", rows_all, grad_pre, preferred_element_type=F32)
    grad_back = jnp.einsum("gecf,gecd->efd", hidden, grad_all, preferred_element_type=F32)
    gated = (gates * out).astype(BF)
    row = jnp.pad(jnp.sum(dy * out, axis=-1), ((0, 0), (0, 128 - ROWS)))
    row = jnp.concatenate(list(parts3(row)), axis=1)
    grad_rows = grad_rows.at[:, CAP, :384].set(row)
    shape = (groups, local * ROWS, width)
    return grad_rows.reshape(shape), gated.reshape(shape), grad_in, grad_back


def on_device(
    tokens,
    valid,
    experts,
    slots,
    ln1_gain,
    ln1_bias,
    w_qkv,
    w_out,
    ln2_gain,
    ln2_bias,
    w_router,
    w_in,
    w_back,
    cotangent,
):
    images, length, width = tokens.shape
    token_count = images * length
    expert_count = w_in.shape[0]
    groups = lax.axis_size("dp") * lax.axis_size("seq")
    members = lax.axis_size("weight")
    devices = groups * members
    local = expert_count // groups
    alone = local == members
    first = (lax.axis_index("dp") * lax.axis_size("seq") + lax.axis_index("seq")) * local
    w_in_mine = lax.dynamic_slice_in_dim(w_in, first, local, 0)
    w_back_mine = lax.dynamic_slice_in_dim(w_back, first, local, 0)
    if alone:
        w_in_mine = exchange(w_in_mine, "weight")
        w_back_mine = exchange(w_back_mine, "weight")

    kept = slots < CAP
    flat = jnp.where(kept, experts * ROWS + slots, -1)
    col = jnp.concatenate(
        [experts, slots, valid[:, :, None], jnp.zeros_like(valid)[:, :, None], flat], axis=2
    )
    row = jnp.swapaxes(col, 1, 2)
    padded = -(-(token_count + expert_count) // 128) * 128
    spare = jnp.arange(expert_count, dtype=jnp.int32) * ROWS + CAP
    index = jnp.concatenate(
        [
            flat.reshape(token_count, TOP).T,
            jnp.stack([spare, jnp.full_like(spare, -1)]),
            jnp.full((TOP, padded - token_count - expert_count), -1, jnp.int32),
        ],
        axis=1,
    )
    gain1, bias1, gain2, bias2 = (
        v.reshape(1, width) for v in (ln1_gain, ln1_bias, ln2_gain, ln2_bias)
    )
    chunk = 8 if expert_count % 8 == 0 else 1
    buffer_shape = jax.ShapeDtypeStruct((expert_count, ROWS, width), BF)
    flat_scratch = pltpu.VMEM((padded, width), F32)

    dy_rows = pl.pallas_call(
        functools.partial(send_kernel, images=images, length=length, chunk=chunk),
        out_shape=buffer_shape,
        scratch_shapes=[flat_scratch],
        compiler_params=PARAMS,
        name="send_dy",
    )(index, cotangent)

    rows_shape = (devices, ROWS, width) if alone else (groups, local * ROWS, width)
    route = EVERY if alone else GROUP
    dy_rows = exchange(dy_rows.reshape(rows_shape), route)

    qkv, ctx, mid, rows, att_squares = pl.pallas_call(
        functools.partial(
            forward_kernel, images=images, length=length, experts=expert_count, chunk=chunk
        ),
        grid=(images,),
        in_specs=[
            per_image(tokens),
            per_image(col),
            per_image(row),
            whole(index),
            whole(gain1),
            whole(bias1),
            whole(w_qkv),
            whole(w_out),
            whole(gain2),
            whole(bias2),
            whole(w_router),
        ],
        out_specs=[
            pl.BlockSpec((1, length, 3 * width), lambda i: (i, 0, 0)),
            pl.BlockSpec((1, length, width), lambda i: (i, 0, 0)),
            pl.BlockSpec((1, length, width), lambda i: (i, 0, 0)),
            whole_out((expert_count, ROWS, width)),
            whole_out((1, width)),
        ],
        out_shape=[
            jax.ShapeDtypeStruct((images, length, 3 * width), BF),
            jax.ShapeDtypeStruct((images, length, width), BF),
            jax.ShapeDtypeStruct((images, length, width), F32),
            buffer_shape,
            jax.ShapeDtypeStruct((1, width), F32),
        ],
        scratch_shapes=[flat_scratch, pltpu.VMEM((expert_count, 128), F32)],
        compiler_params=PARAMS,
        name="forward",
    )(tokens, col, row, index, gain1, bias1, w_qkv, w_out, gain2, bias2, w_router)

    rows = exchange(rows.reshape(rows_shape), route)
    if alone:
        grad_rows, gated, grads = experts_here(rows, dy_rows, w_in_mine, w_back_mine)
    else:
        grad_rows, gated, grad_in, grad_back = experts_split(
            rows, dy_rows, w_in_mine, w_back_mine, groups
        )
    back_shape = (expert_count * ROWS, width)
    grad_rows = exchange(grad_rows, route).reshape(back_shape)
    gated = exchange(gated, route).reshape(back_shape)
    if alone:
        grads = exchange(grads, "weight").astype(F32)
        grad_in = grads[:, :width]
        grad_back = grads[:, width:]

    packed = 4 * width + -(-expert_count // 128) * 128
    grad_tokens, weight_sums, norm_sums = pl.pallas_call(
        functools.partial(backward_kernel, images=images, length=length, experts=expert_count),
        grid=(images,),
        in_specs=[
            whole(grad_rows),
            per_image(tokens),
            per_image(mid),
            per_image(cotangent),
            per_image(qkv),
            per_image(ctx),
            per_image(col),
            whole(gain1),
            whole(bias1),
            whole(w_qkv),
            whole(w_out),
            whole(gain2),
            whole(bias2),
            whole(w_router),
        ],
        out_specs=[
            pl.BlockSpec((1, length, width), lambda i: (i, 0, 0)),
            whole_out((width, packed)),
            whole_out((4, width)),
        ],
        out_shape=[
            jax.ShapeDtypeStruct((images, length, width), BF),
            jax.ShapeDtypeStruct((width, packed), BF),
            jax.ShapeDtypeStruct((4, width), F32),
        ],
        scratch_shapes=[
            pltpu.VMEM((width, 3 * width), F32),
            pltpu.VMEM((width, width), F32),
            pltpu.VMEM((width, expert_count), F32),
            pltpu.VMEM((expert_count, 128), F32),
            pltpu.VMEM((length, 3 * width), BF),
        ],
        compiler_params=PARAMS,
        name="backward",
    )(
        grad_rows,
        tokens,
        mid,
        cotangent,
        qkv,
        ctx,
        col,
        gain1,
        bias1,
        w_qkv,
        w_out,
        gain2,
        bias2,
        w_router,
    )

    output, moe_squares = pl.pallas_call(
        final_kernel,
        grid=(images,),
        in_specs=[whole(gated), per_image(mid), per_image(col)],
        out_specs=[
            pl.BlockSpec((1, length, width), lambda i: (i, 0, 0)),
            whole_out((2, width)),
        ],
        out_shape=[
            jax.ShapeDtypeStruct((images, length, width), BF),
            jax.ShapeDtypeStruct((2, width), F32),
        ],
        compiler_params=PARAMS,
        name="final",
    )(gated, mid, col)

    plane = lax.axis_size("dp") * members
    depth = lax.axis_size("seq")
    share = width // plane
    total = exchange(weight_sums.reshape(plane, share, packed), PLANE)
    total = jnp.sum(total.astype(F32), axis=0).astype(BF)
    total = exchange(total.reshape(depth, share // depth, packed), "seq")
    total = jnp.sum(total.astype(F32), axis=0).astype(BF)
    total = exchange(jnp.broadcast_to(total[None], (depth,) + total.shape), "seq")
    total = total.reshape(share, packed)
    total = exchange(jnp.broadcast_to(total[None], (plane,) + total.shape), PLANE)
    total = total.reshape(width, packed).astype(F32)

    small = jnp.concatenate(
        [norm_sums, att_squares, moe_squares, jnp.zeros((1, width), F32)], axis=0
    )
    small = exchange(jnp.broadcast_to(small[None], (devices,) + small.shape), EVERY)
    small = jnp.sum(small, axis=0)
    rms_values = jnp.sqrt(
        jnp.sum(small[4:7], axis=1) / float(images * devices * VALID * width)
    )
    return (
        output,
        grad_tokens,
        small[0],
        small[1],
        total[:, : 3 * width],
        total[:, 3 * width : 4 * width],
        small[2],
        small[3],
        total[:, 4 * width : 4 * width + expert_count],
        grad_in,
        grad_back,
        rms_values,
    )


def solution(mesh):
    spread = P(("dp", "seq", "weight"), None, None)
    placed = (
        spread,
        P(("dp", "seq", "weight"), None),
        spread,
        spread,
        P(),
        P(),
        P(),
        P(),
        P(),
        P(),
        P(),
        P(None, None, "weight"),
        P(None, "weight", None),
        spread,
    )
    return jax.shard_map(
        on_device,
        mesh=mesh,
        in_specs=placed,
        out_specs=(
            spread,
            spread,
            P(),
            P(),
            P(),
            P(),
            P(),
            P(),
            P(),
            P(("dp", "seq"), None, "weight"),
            P(("dp", "seq"), "weight", None),
            P(),
        ),
        check_vma=False,
    )
```

time: 1280 us -> 423 us (0.33)
  waiting for transfers between devices: 853 us -> 183 us
  matrix products: 155 us -> 0 us
  local copies, waits for them, and re-layouts: 120 us -> 24.3 us
  Pallas kernels: 0 us -> 79.1 us
  other arithmetic: 64.2 us -> 3.78 us
  blocking collectives: 38.5 us -> 95.2 us
  between operations: 15.2 us -> 0.89 us
    reduce_scatter x4 -> x0, waiting for transfers between devices: 408 us -> none  [the longest x1 278 us: on_device(): lax.psum_scatter(grad_back_part.astype(jnp.bfloat16), ('dp', 'seq'), scat...]
    dot_general x21 -> x0, matrix products: 155 us -> none  [the longest x1 29.1 us: on_device(): jnp.einsum('ced,efd->cef', out_grads, w_back, preferred_element_type=jnp....]
    psum x1 -> x0, waiting for transfers between devices: 146 us -> none  [on_device(): lax.psum((grad_qkv_part, grad_out_part, grad_router_part, norm_grads, squ...]
    all_to_all x0 -> x3, blocking collectives: none -> 95.2 us  [exchange(): return lax.all_to_all(v, axes, split_axis=0, concat_axis=0, tiled=True)]
    all_gather x2 -> x0, waiting for transfers between devices: 90.3 us -> none  [the longest x1 45.7 us: on_device(): out_grads = lax.all_gather(grad_slots, 'weight', axis=0, tiled=True)]
    pallas_call x0 -> x6, Pallas kernels: none -> 79.1 us  [the longest x1 22 us: experts_here(): pl.pallas_call(expert_kernel, grid=(devices // step,), in_specs=[block3,...]
    psum x1 -> x0, blocking collectives: 38.5 us -> none  [on_device(): lax.psum((grad_qkv_part, grad_out_part, grad_router_part, norm_grads, squ...]
    all_to_all x5 -> x9, waiting for transfers between devices: 209 us -> 183 us  [exchange(): return lax.all_to_all(v, axes, split_axis=0, concat_axis=0, tiled=True)]
  transfers between devices with their start and end apart: 12 -> 9, of which waited for: 11 -> 9; matrix products, arithmetic and copies ran while one was open for 14% -> 4% of each run, Pallas kernels for 0% -> 14%
where the time goes in v1:
time: 423 us; the launch traced here: 422 us
  waiting for transfers between devices  183 us (43%)
  blocking collectives  95.2 us (23%)
  Pallas kernels  79.1 us (19%)
  starting transfers between devices  35.5 us (8%)
  local copies, waits for them, and re-layouts  24.3 us (6%)
    all_to_all x9, waiting for transfers between devices, exchange(): return lax.all_to_all(v, axes, split_axis=0, concat_axis=0, tiled=True)  183 us
    all_to_all x3, blocking collectives, exchange(): return lax.all_to_all(v, axes, split_axis=0, concat_axis=0, tiled=True)  95.2 us
    all_to_all x9, starting transfers between devices, exchange(): return lax.all_to_all(v, axes, split_axis=0, concat_axis=0, tiled=True)  35.5 us
    pallas_call x1, Pallas kernels, experts_here(): pl.pallas_call(expert_kernel, grid=(devices // step,), in_specs=[block3,...  22 us
    pallas_call x1, Pallas kernels, on_device(): pl.pallas_call(functools.partial(backward_kernel, images=images, length=l...  21.8 us
    pallas_call x1, Pallas kernels, on_device(): pl.pallas_call(functools.partial(forward_kernel, images=images, length=le...  14.6 us
    pallas_call x1, Pallas kernels, experts_here(): pl.pallas_call(expert_weights_kernel, grid=(pieces,), in_specs=[whole(row...  11.7 us
  transfers between devices with their start and end apart: 9, of which 9 were waited for; matrix products, arithmetic and copies ran while one was open for 4% of the time, Pallas kernels for 14%

profile of v1, /device:TPU:0, one launch (start us, length us, event | category | flops | bytes accessed | tf_op | source)
XLA Modules:
  0.0 421.8 jit_solution(10737918807609164184)
XLA Ops:
  0.6 3.0 constant_dynamic-slice_fusion.1
  3.7 4.2 %all-to-all-start.2 = ((bf16[4,512,512]{2,1,0:T(8,128)(2,1)}), bf16[4,512,512]{2,1,0:T(8,128)(2,1)S(1)}, u32[]{:S(2)}, u32[]{:S(2)}) async-start(bf16[4,512,512]{2,1,0:T(8,128)(2,1)} %constant_dynamic-slice_fusion.1), calls=%async_computation.2 | async-start | bytes 4194304 | tf_op jit(solution)/shard_map/all_to_all | solution.py:419
  7.9 3.0 constant_dynamic-slice_fusion
  11.0 22.6 %all-to-all-done.2.w_in_ref = bf16[4,512,512]{2,1,0:T(8,128)(2,1)S(1)} async-done(((bf16[4,512,512]{2,1,0:T(8,128)(2,1)}), bf16[4,512,512]{2,1,0:T(8,128)(2,1)S(1)}, u32[]{:S(2)}, u32[]{:S(2)}) %all-to-all-start.2) | async-done | bytes 2097184 | tf_op jit(solution)/shard_map/all_to_all | solution.py:419
  33.6 4.5 %all-to-all-start.3 = ((bf16[4,512,512]{2,1,0:T(8,128)(2,1)}), bf16[4,512,512]{2,1,0:T(8,128)(2,1)}, u32[]{:S(2)}, u32[]{:S(2)}) async-start(bf16[4,512,512]{2,1,0:T(8,128)(2,1)} %constant_dynamic-slice_fusion), calls=%async_computation.3 | async-start | bytes 4194304 | tf_op jit(solution)/shard_map/all_to_all | solution.py:419
  38.1 0.2 copy.85
  38.5 0.2 copy.81
  38.7 0.2 copy.83
  39.2 0.4 concatenate.9.col_ref
  39.7 0.7 copy.88.row_ref
  40.6 0.8 copy.89.w_router_ref
  41.4 0.7 fusion.1.index_ref
  42.1 14.6 %forward.1 = (bf16[3,200,1536]{2,1,0:T(8,128)(2,1)}, bf16[3,200,512]{2,1,0:T(8,128)(2,1)}, f32[3,200,512]{2,1,0:T(8,128)}, bf16[32,48,512]{2,1,0:T(8,128)(2,1)}, f32[1,512]{1,0:T(1,128)}) custom-call(bf16[3,200,512]{2,1,0:T(8,128)(2,1)} %x_ref.3, s32[3,200,8]{2,1,0:T(8,128)} %copy-done.1, s32[3,8,200]{2,1,0:T(8,128)} %copy.88.row_ref, ...), custom_call_target="tpu_custom_call" | custom-call | tf_op jit(solution)/shard_map/forward/pallas_call | solution.py:558
  56.7 7.1 %all-to-all-done.3.w_back_ref = bf16[4,512,512]{2,1,0:T(8,128)(2,1)} async-done(((bf16[4,512,512]{2,1,0:T(8,128)(2,1)}), bf16[4,512,512]{2,1,0:T(8,128)(2,1)}, u32[]{:S(2)}, u32[]{:S(2)}) %all-to-all-start.3) | async-done | bytes 2097184 | tf_op jit(solution)/shard_map/all_to_all | solution.py:419
  63.9 5.7 %all-to-all-start = ((bf16[32,48,512]{2,1,0:T(8,128)(2,1)}), bf16[32,48,512]{2,1,0:T(8,128)(2,1)S(1)}, u32[]{:S(2)}, u32[]{:S(2)}) async-start(bf16[32,48,512]{2,1,0:T(8,128)(2,1)} %get-tuple-element.28), calls=%async_computation | async-start | bytes 3145728 | tf_op jit(solution)/shard_map/all_to_all | solution.py:419
  69.6 4.2 send_dy.1
  73.8 34.2 %all-to-all-done.rows_ref = bf16[32,48,512]{2,1,0:T(8,128)(2,1)S(1)} async-done(((bf16[32,48,512]{2,1,0:T(8,128)(2,1)}), bf16[32,48,512]{2,1,0:T(8,128)(2,1)S(1)}, u32[]{:S(2)}, u32[]{:S(2)}) %all-to-all-start) | async-done | bytes 1572896 | tf_op jit(solution)/shard_map/all_to_all | solution.py:419
  108.0 41.8 %all_to_all.60.dy_ref = bf16[32,48,512]{2,1,0:T(8,128)(2,1)} all-to-all(bf16[32,48,512]{2,1,0:T(8,128)(2,1)} %send_dy.1), channel_id=1, replica_groups=mesh['dp'=2,'seq'=4,'weight'=4] {'dp','seq','weight'}, dimensions={0} | all-to-all | bytes 3145728 | tf_op jit(solution)/shard_map/all_to_all | solution.py:419
  149.8 22.0 %experts.1 = (bf16[32,48,512]{2,1,0:T(8,128)(2,1)}, bf16[32,48,512]{2,1,0:T(8,128)(2,1)}, bf16[1536,512]{1,0:T(8,128)(2,1)}, bf16[1536,512]{1,0:T(8,128)(2,1)}, ...) custom-call(bf16[32,48,512]{2,1,0:T(8,128)(2,1)} %copy-done.3, bf16[32,48,512]{2,1,0:T(8,128)(2,1)} %all_to_all.60.dy_ref, ...), custom_call_target="tpu_custom_call" | custom-call | tf_op jit(solution)/shard_map/experts/pallas_call | solution.py:431
  171.9 41.8 %all_to_all.61 = bf16[32,48,512]{2,1,0:T(8,128)(2,1)} all-to-all(bf16[32,48,512]{2,1,0:T(8,128)(2,1)} %get-tuple-element.32), channel_id=1, replica_groups=mesh['dp'=2,'seq'=4,'weight'=4] {'dp','seq','weight'}, dimensions={0} | all-to-all | bytes 3145728 | tf_op jit(solution)/shard_map/all_to_all | solution.py:419
  213.7 2.9 all-to-all-start.4
  216.6 21.8 %backward.1 = (bf16[3,200,512]{2,1,0:T(8,128)(2,1)}, bf16[512,2176]{1,0:T(8,128)(2,1)}, f32[4,512]{1,0:T(4,128)}) custom-call(bf16[1536,512]{1,0:T(8,128)(2,1)} %bitcast.23, bf16[3,200,512]{2,1,0:T(8,128)(2,1)} %x_ref.3, f32[3,200,512]{2,1,0:T(8,128)} %get-tuple-element.30.mid_ref, bf16[3,200,512]{2,1,0:T(8,128)(2,1)} %dy_ref.1, ...), custom_call_target="tpu_custom_call" | custom-call | tf_op jit(solution)/shard_map/backward/pallas_call | solution.py:611
  238.4 16.4 %all-to-all-done.4 = bf16[32,48,512]{2,1,0:T(8,128)(2,1)S(1)} async-done(((bf16[32,48,512]{2,1,0:T(8,128)(2,1)}), bf16[32,48,512]{2,1,0:T(8,128)(2,1)S(1)}, u32[]{:S(2)}, u32[]{:S(2)}) %all-to-all-start.4) | async-done | bytes 1572896 | tf_op jit(solution)/shard_map/all_to_all | solution.py:419
  254.8 1.1 copy-done.2
  255.9 3.6 all-to-all-start.7
  259.5 11.7 %expert_weights.1 = bf16[4,1024,512]{2,1,0:T(8,128)(2,1)} custom-call(bf16[1536,512]{1,0:T(8,128)(2,1)} %get-tuple-element.40.rows_ref, bf16[1536,512]{1,0:T(8,128)(2,1)} %get-tuple-element.41.grad_out_ref, bf16[1536,2048]{1,0:T(8,128)(2,1)} %get-tuple-element.42.hidden_ref, bf16[1536,2048]{1,0:T(8,128)(2,1)} %get-tuple-element.43.grad_pre_ref), custom_call_target="tpu_custom_call" | custom-call | tf_op jit(solution)/shard_map/expert_weights/pallas_call | solution.py:448
  271.3 16.2 %all-to-all-done.7 = bf16[8,64,2176]{2,1,0:T(8,128)(2,1)S(1)} async-done(((bf16[8,64,2176]{2,1,0:T(8,128)(2,1)}), bf16[8,64,2176]{2,1,0:T(8,128)(2,1)S(1)}, u32[]{:S(2)}, u32[]{:S(2)}) %all-to-all-start.7) | async-done | bytes 2228256 | tf_op jit(solution)/shard_map/all_to_all | solution.py:419
  287.5 4.9 %all-to-all-start.11 = ((bf16[4,1024,512]{2,1,0:T(8,128)(2,1)}), bf16[4,1024,512]{2,1,0:T(8,128)(2,1)}, u32[]{:S(2)}, u32[]{:S(2)}) async-start(bf16[4,1024,512]{2,1,0:T(8,128)(2,1)} %expert_weights.1), calls=%async_computation.11 | async-start | bytes 8388608 | tf_op jit(solution)/shard_map/all_to_all | solution.py:419
  292.4 1.1 reduce_sum.43
  293.5 47.1 %all-to-all-done.11 = bf16[4,1024,512]{2,1,0:T(8,128)(2,1)} async-done(((bf16[4,1024,512]{2,1,0:T(8,128)(2,1)}), bf16[4,1024,512]{2,1,0:T(8,128)(2,1)}, u32[]{:S(2)}, u32[]{:S(2)}) %all-to-all-start.11) | async-done | bytes 4194336 | tf_op jit(solution)/shard_map/all_to_all | solution.py:419
  340.6 3.5 all-to-all-start.8
  344.1 4.7 %final.1 = (bf16[3,200,512]{2,1,0:T(8,128)(2,1)}, f32[2,512]{1,0:T(2,128)}) custom-call(bf16[1536,512]{1,0:T(8,128)(2,1)} %bitcast.22, f32[3,200,512]{2,1,0:T(8,128)} %get-tuple-element.30.mid_ref, s32[3,200,8]{2,1,0:T(8,128)} %copy-done.1), custom_call_target="tpu_custom_call" | custom-call | tf_op jit(solution)/shard_map/final/pallas_call | solution.py:666
  348.8 0.8 maximum_maximum_fusion
  349.6 3.7 all-to-all-done.8
  353.2 0.9 broadcast_in_dim.32
  354.1 2.6 all-to-all-start.6
  356.8 15.8 %all-to-all-done.6 = f32[32,8,512]{2,1,0:T(8,128)S(1)} async-done(((f32[32,8,512]{2,1,0:T(8,128)}), f32[32,8,512]{2,1,0:T(8,128)S(1)}, u32[]{:S(2)}, u32[]{:S(2)}) %all-to-all-start.6) | async-done | bytes 524320 | tf_op jit(solution)/shard_map/all_to_all | solution.py:419
  372.6 11.6 %all_to_all.62 = bf16[4,16,2176]{2,1,0:T(8,128)(2,1)S(1)} all-to-all(bf16[4,16,2176]{2,1,0:T(8,128)(2,1)S(1)} %broadcast_in_dim.33), channel_id=1, replica_groups=mesh['dp'=2,'seq'=4,'weight'=4] {'seq'}, dimensions={0} | all-to-all | bytes 557056 | tf_op jit(solution)/shard_map/all_to_all | solution.py:419
  384.2 1.6 broadcast_in_dim.35
  385.8 3.6 all-to-all-start.10
  389.4 6.8 %fusion.2 = (f32[4,512,512]{2,1,0:T(8,128)}, f32[4,512,512]{2,1,0:T(8,128)}) fusion(bf16[4,1024,512]{2,1,0:T(8,128)(2,1)} %all-to-all-done.11), kind=kLoop, calls=%fused_computation.13 | loop fusion | bytes 16777216 | tf_op jit(solution)/shard_map/slice | solution.py:608
  396.4 0.5 multiply_sqrt_fusion
  396.9 0.6 fusion.3
  397.5 19.9 %all-to-all-done.10 = bf16[8,64,2176]{2,1,0:T(8,128)(2,1)S(1)} async-done(((bf16[8,64,2176]{2,1,0:T(8,128)(2,1)}), bf16[8,64,2176]{2,1,0:T(8,128)(2,1)S(1)}, u32[]{:S(2)}, u32[]{:S(2)}) %all-to-all-start.10) | async-done | bytes 2228256 | tf_op jit(solution)/shard_map/all_to_all | solution.py:419
  417.4 0.5 bitcast_convert_fusion
  417.8 2.1 slice.42
  419.9 1.1 slice.43
  421.1 0.7 copy.91
  (35 shorter events, 1.0 us)
Async XLA Ops:
  3.7 29.9 %all-to-all-start.2 = ((bf16[4,512,512]{2,1,0:T(8,128)(2,1)}), bf16[4,512,512]{2,1,0:T(8,128)(2,1)S(1)}, u32[]{:S(2)}, u32[]{:S(2)}) async-start(bf16[4,512,512]{2,1,0:T(8,128)(2,1)} %constant_dynamic-slice_fusion.1), calls=%async_computation.2 | async-start | bytes 4194304 | tf_op jit(solution)/shard_map/all_to_all | solution.py:419
  11.0 27.2 %copy-start.6 = (s32[3,200,2]{1,2,0:T(2,128)S(1)}, s32[3,200,2]{1,2,0:T(2,128)}, u32[]{:S(2)}) copy-start(s32[3,200,2]{1,2,0:T(2,128)} %param.17) | copy-start | bytes 14404
  11.0 27.3 %copy-start.5 = (s32[3,200,2]{1,2,0:T(2,128)S(1)}, s32[3,200,2]{1,2,0:T(2,128)}, u32[]{:S(2)}) copy-start(s32[3,200,2]{1,2,0:T(2,128)} %param.16) | copy-start | bytes 14404
  11.0 28.0 %copy-start.8 = (s32[3,200]{1,0:T(4,128)S(1)}, s32[3,200]{1,0:T(4,128)}, u32[]{:S(2)}) copy-start(s32[3,200]{1,0:T(4,128)} %param.15) | copy-start | bytes 7204
  33.6 4.7 %copy-start = (bf16[4,512,512]{2,1,0:T(8,128)(2,1)}, bf16[4,512,512]{2,1,0:T(8,128)(2,1)S(1)}, u32[]{:S(2)}) copy-start(bf16[4,512,512]{2,1,0:T(8,128)(2,1)S(1)} %all-to-all-done.2.w_in_ref) | copy-start | bytes 6291460
  33.6 30.2 %all-to-all-start.3 = ((bf16[4,512,512]{2,1,0:T(8,128)(2,1)}), bf16[4,512,512]{2,1,0:T(8,128)(2,1)}, u32[]{:S(2)}, u32[]{:S(2)}) async-start(bf16[4,512,512]{2,1,0:T(8,128)(2,1)} %constant_dynamic-slice_fusion), calls=%async_computation.3 | async-start | bytes 4194304 | tf_op jit(solution)/shard_map/all_to_all | solution.py:419
  38.5 2.1 copy-start.4
  39.7 2.4 copy-start.1
  63.9 44.1 %all-to-all-start = ((bf16[32,48,512]{2,1,0:T(8,128)(2,1)}), bf16[32,48,512]{2,1,0:T(8,128)(2,1)S(1)}, u32[]{:S(2)}, u32[]{:S(2)}) async-start(bf16[32,48,512]{2,1,0:T(8,128)(2,1)} %get-tuple-element.28), calls=%async_computation | async-start | bytes 3145728 | tf_op jit(solution)/shard_map/all_to_all | solution.py:419
  108.0 41.8 %copy-start.3 = (bf16[32,48,512]{2,1,0:T(8,128)(2,1)}, bf16[32,48,512]{2,1,0:T(8,128)(2,1)S(1)}, u32[]{:S(2)}) copy-start(bf16[32,48,512]{2,1,0:T(8,128)(2,1)S(1)} %all-to-all-done.rows_ref) | copy-start | bytes 4718596
  213.7 41.1 %all-to-all-start.4 = ((bf16[32,48,512]{2,1,0:T(8,128)(2,1)}), bf16[32,48,512]{2,1,0:T(8,128)(2,1)S(1)}, u32[]{:S(2)}, u32[]{:S(2)}) async-start(bf16[32,48,512]{2,1,0:T(8,128)(2,1)} %get-tuple-element.29), calls=%async_computation.4 | async-start | bytes 3145728 | tf_op jit(solution)/shard_map/all_to_all | solution.py:419
  254.8 1.1 copy-start.2
  255.9 31.6 %all-to-all-start.7 = ((bf16[8,64,2176]{2,1,0:T(8,128)(2,1)}), bf16[8,64,2176]{2,1,0:T(8,128)(2,1)S(1)}, u32[]{:S(2)}, u32[]{:S(2)}) async-start(bf16[8,64,2176]{2,1,0:T(8,128)(2,1)} %bitcast.25), calls=%async_computation.7 | async-start | bytes 4456448 | tf_op jit(solution)/shard_map/all_to_all | solution.py:419
  287.5 53.1 %all-to-all-start.11 = ((bf16[4,1024,512]{2,1,0:T(8,128)(2,1)}), bf16[4,1024,512]{2,1,0:T(8,128)(2,1)}, u32[]{:S(2)}, u32[]{:S(2)}) async-start(bf16[4,1024,512]{2,1,0:T(8,128)(2,1)} %expert_weights.1), calls=%async_computation.11 | async-start | bytes 8388608 | tf_op jit(solution)/shard_map/all_to_all | solution.py:419
  293.4 55.3 %copy-start.7 = (f32[4,512]{1,0:T(4,128)S(1)}, f32[4,512]{1,0:T(4,128)}, u32[]{:S(2)}) copy-start(f32[4,512]{1,0:T(4,128)} %get-tuple-element.36) | copy-start | bytes 24580
  293.5 55.3 %copy-start.9 = (f32[1,512]{1,0:T(1,128)S(1)}, f32[1,512]{1,0:T(1,128)}, u32[]{:S(2)}) copy-start(f32[1,512]{1,0:T(1,128)} %get-tuple-element.37) | copy-start | bytes 6148
  340.6 12.7 %all-to-all-start.8 = ((bf16[4,16,2176]{2,1,0:T(8,128)(2,1)}), bf16[4,16,2176]{2,1,0:T(8,128)(2,1)S(1)}, u32[]{:S(2)}, u32[]{:S(2)}) async-start(bf16[4,16,2176]{2,1,0:T(8,128)(2,1)} %bitcast.13), calls=%async_computation.8 | async-start | bytes 557056 | tf_op jit(solution)/shard_map/all_to_all | solution.py:419
  354.1 18.5 %all-to-all-start.6 = ((f32[32,8,512]{2,1,0:T(8,128)}), f32[32,8,512]{2,1,0:T(8,128)S(1)}, u32[]{:S(2)}, u32[]{:S(2)}) async-start(f32[32,8,512]{2,1,0:T(8,128)} %broadcast_in_dim.32), calls=%async_computation.6 | async-start | bytes 1048576 | tf_op jit(solution)/shard_map/all_to_all | solution.py:419
  385.8 31.6 %all-to-all-start.10 = ((bf16[8,64,2176]{2,1,0:T(8,128)(2,1)}), bf16[8,64,2176]{2,1,0:T(8,128)(2,1)S(1)}, u32[]{:S(2)}, u32[]{:S(2)}) async-start(bf16[8,64,2176]{2,1,0:T(8,128)(2,1)} %broadcast_in_dim.35), calls=%async_computation.10 | async-start | bytes 4456448 | tf_op jit(solution)/shard_map/all_to_all | solution.py:419
